TPU v7x, 32 devices: a whole 2x2x4 slice. The times are simulated.
32 devices in a mesh: blk: 4 (over y, x), team: 4 (over z), dp: 2 (over core).
Axes of the slice: x: 2, y: 2, z: 4, core: 2. Of those that a mesh axis runs over, the one named last changes fastest.
Arguments:
- hidden: bfloat16 [1024, 28672], P(('blk', 'dp'), 'team'), may hold values from -6 to 6
- out_grad: bfloat16 [1024, 8192], P(('blk', 'dp'), 'team'), may hold values from -0.1875 to 0.1875
- act_rows: int32 [4, 64, 12], P('team'), may hold values from 0 to 55, as said below
- col_owner: int32 [64], replicated, may hold values from 0 to 3, as said below
Outputs:
- gradients: float32 [4, 4, 288, 128, 128], P('team', 'blk', 'dp')
- scores: float32 [4, 4, 288], P('team', 'blk', 'dp')
Inputs may be any that keep to these rules, and one draw needn't show every extreme that they name: For each t and c the 12 entries act_rows[t, c, :] are distinct. `col_owner`: some owner holds exactly 24 block columns and no owner holds more.
All inputs are finite; a program needn't handle non-finite values.
Results may differ from a plain program's by a relative error of at most 0.0003.
Values may be sent and summed in bfloat16 or wider, within the bound.
A program may use at most 192 MiB of HBM per device.

v0:
```python
import jax
import jax.numpy as jnp
from jax import lax
from jax.sharding import PartitionSpec as P

D = 8192
BS = 128
epsilon = 1e-06


def on_device(hidden, out_grad, act_rows, col_owner):
    owners_count = lax.axis_size("blk")
    owner_index = lax.axis_index("blk")
    column_blocks = D // BS
    capacity = min(3 * column_blocks // (2 * owners_count), 3 * column_blocks // 4)
    per_column = act_rows.shape[2]
    owners = jnp.arange(owners_count, dtype=jnp.int32)
    onehot = (col_owner[:, None] == owners[None, :]).astype(jnp.int32)
    column_rank = jnp.sum((jnp.cumsum(onehot, axis=0) - onehot) * onehot, axis=1)
    slot_ids = jnp.arange(capacity, dtype=jnp.int32)
    matches = (col_owner[None, None, :] == owners[:, None, None]) & (
        column_rank[None, None, :] == slot_ids[None, :, None]
    )
    owned_all = jnp.sum(
        matches.astype(jnp.int32) * jnp.arange(column_blocks, dtype=jnp.int32)[None, None, :],
        axis=2,
    )
    alive_all = jnp.any(matches, axis=2)
    owned_mine = lax.dynamic_index_in_dim(owned_all, owner_index, 0, keepdims=False)
    alive_mine = lax.dynamic_index_in_dim(alive_all, owner_index, 0, keepdims=False)
    block_rows = jnp.take(act_rows[0], owned_mine, axis=0).reshape(-1)
    grad_full = lax.all_gather(out_grad, "team", axis=1, tiled=True)
    grad_mask = alive_mine.astype(jnp.bfloat16)[None, :, None]
    hidden_piece = lax.all_gather(hidden, "blk", axis=0, tiled=True)
    grad_piece = lax.all_gather(grad_full, "blk", axis=0, tiled=True)
    count_rows = grad_piece.shape[0]
    picked_grad = (
        jnp.take(grad_piece.reshape(count_rows, column_blocks, BS), owned_mine, axis=1) * grad_mask
    )
    count_rows = hidden_piece.shape[0]
    hidden_blocks = hidden_piece.reshape(count_rows, -1, BS)
    picked_hidden = jnp.take(hidden_blocks, block_rows, axis=1).reshape(
        count_rows, capacity, per_column, BS
    )
    partial_value = jnp.einsum(
        "ncki,ncj->ckij", picked_hidden, picked_grad, preferred_element_type=jnp.float32
    )
    partial_value = partial_value.reshape(capacity * per_column, BS, BS)
    gradients = lax.psum_scatter(partial_value, "dp", scatter_dimension=0, tiled=True)
    scores = jnp.sqrt(jnp.mean(gradients * gradients, axis=(1, 2)) + epsilon)
    return (gradients[None, None], scores[None, None])


def solution(mesh):
    in_specs = (P(("blk", "dp"), "team"), P(("blk", "dp"), "team"), P("team", None, None), P())
    out_specs = (P("team", "blk", "dp", None, None), P("team", "blk", "dp"))
    return jax.shard_map(
        on_device, mesh=mesh, in_specs=in_specs, out_specs=out_specs, check_vma=False
    )
```

profile of v0, /device:TPU:0, one launch (start us, length us, event | category | flops | bytes accessed | tf_op | source)
XLA Modules:
  0.0 305.4 jit_solution(6852745690831261006)
XLA Ops:
  7.2 0.0 copy-start.1
  7.2 0.0 all-gather.6.cloned.1.call-start
  7.2 2.0 copy.20
  9.3 0.0 all-gather.6.cloned.1.call-update
  9.3 0.0 all-gather.4.cloned.1.call-start
  9.3 3.9 %copy.17 = bf16[128,7168]{0,1:T(8,128)(2,1)} copy(bf16[128,7168]{1,0:T(8,128)(2,1)} %param.4) | data formatting | bytes 3670016 | tf_op args[0]
  13.2 0.0 all-gather.4.cloned.1.call-update
  13.2 0.0 all-gather.8.cloned.1.call-start
  13.3 44.7 %all-gather.6.cloned.1.call-done = bf16[128,8192]{0,1:T(8,128)(2,1)} async-done(((bf16[128,2048]{0,1:T(8,128)(2,1)}), bf16[128,8192]{0,1:T(8,128)(2,1)}) %all-gather.6.cloned.1.call-update) | async-done | bytes 2097168 | tf_op jit(solution)/shard_map/all_gather | solution.py:32
  58.0 0.0 all-gather.8.cloned.1.call-update
  58.0 0.0 reduce-scatter.2.cloned.1.call-start
  58.1 0.1 fusion.11
  58.1 0.1 reduce_window_sum.11
  58.2 0.1 copy.16
  58.3 0.2 select_reduce_fusion
  58.5 0.1 fusion.10
  58.7 0.6 gather_fusion
  59.3 0.1 compare_and_fusion
  59.4 0.1 select_n.73
  59.5 0.2 and_reduce_fusion
  59.7 78.1 %all-gather.4.cloned.1.call-done = bf16[512,7168]{0,1:T(8,128)(2,1)} async-done(((bf16[128,7168]{0,1:T(8,128)(2,1)}), bf16[512,7168]{0,1:T(8,128)(2,1)}) %all-gather.4.cloned.1.call-update) | async-done | bytes 7340048 | tf_op jit(solution)/shard_map/all_gather | solution.py:34
  137.8 10.4 %copy.18 = bf16[512,56,128]{2,0,1:T(8,128)(2,1)} copy(bf16[512,56,128]{0,2,1:T(8,128)(2,1)} %bitcast.28) | data formatting | bytes 14680064 | tf_op jit(solution)/shard_map/reshape | solution.py:41
  148.3 18.8 %gather_fusion.1 = bf16[288,512,128]{2,1,0:T(8,128)(2,1)} fusion(bf16[512,56,128]{2,0,1:T(8,128)(2,1)} %copy.18, s32[1024]{0:T(1024)S(1)} %pad_clamp_fusion), kind=kCustom, calls=%fused_computation.1 | custom fusion | bytes 75498624 | tf_op jit(solution)/shard_map/jit(_take)/gather | solution.py:42
  167.1 48.8 %copy.19 = bf16[512,24,12,128]{0,3,2,1:T(8,128)(2,1)} copy(bf16[512,24,12,128]{3,0,2,1:T(8,128)(2,1)} %bitcast.24) | data formatting | bytes 75497472 | tf_op jit(solution)/shard_map/jit(_take)/gather | solution.py:42
  215.8 11.2 %all-gather.8.cloned.1.call-done = bf16[512,8192]{0,1:T(8,128)(2,1)} async-done(((bf16[128,8192]{0,1:T(8,128)(2,1)}), bf16[512,8192]{0,1:T(8,128)(2,1)}) %all-gather.8.cloned.1.call-update) | async-done | bytes 8388624 | tf_op jit(solution)/shard_map/all_gather | solution.py:35
  227.0 11.9 %copy.21 = bf16[512,64,128]{2,0,1:T(8,128)(2,1)} copy(bf16[512,64,128]{0,2,1:T(8,128)(2,1)} %bitcast.27) | data formatting | bytes 16777216 | tf_op jit(solution)/shard_map/reshape | solution.py:38
  238.9 4.5 %gather_fusion.2 = bf16[24,512,128]{2,1,0:T(8,128)(2,1)S(1)} fusion(bf16[512,64,128]{2,0,1:T(8,128)(2,1)} %copy.21, s32[1024]{0:T(1024)S(1)} %pad_clamp_fusion.1), kind=kCustom, calls=%fused_computation.2 | custom fusion | bytes 6291552 | tf_op jit(solution)/shard_map/jit(_take)/gather | solution.py:38
  243.5 23.4 %fusion = f32[24,12,128,128]{3,2,1,0:T(8,128)} fusion(bf16[512,24,12,128]{0,3,2,1:T(8,128)(2,1)} %copy.19, pred[24,12]{1,0:T(8,128)(4,1)S(1)} %get-tuple-element.2, bf16[24,512,128]{2,1,0:T(8,128)(2,1)S(1)} %gather_fusion.2, pred[24]{0:T(512)(128)(4,1)S(1)} %compare_and_fusion.1, bf16[24]{0:T(256)(128)(2,1)S(1)} %fusion.13), kind=kOutput, calls=%fused_computation.3 | convolution fusion | flops 4853858304 | bytes 59769192 | tf_op jit(solution)/shard_map/ncki,ncj->ckij/dot_general | solution.py:45
  266.8 0.0 reduce-scatter.2.cloned.1.call-update
  266.9 26.7 %reduce-scatter.2.cloned.1.call-done = f32[144,128,128]{2,1,0:T(8,128)} async-done(((f32[288,128,128]{2,1,0:T(8,128)}), f32[144,128,128]{2,1,0:T(8,128)}) %reduce-scatter.2.cloned.1.call-update) | async-done | bytes 9437200 | tf_op jit(solution)/shard_map/reduce_scatter | solution.py:49
  293.6 4.7 %multiply_reduce_fusion = f32[144]{0:T(256)S(1)} fusion(f32[144,128,128]{2,1,0:T(8,128)} %reduce-scatter.2.cloned.1.call-done), kind=kLoop, calls=%fused_computation.7 | loop fusion | flops 4718448 | bytes 9437760 | tf_op jit(solution)/shard_map/reduce_sum | solution.py:50
  298.3 0.6 add_sqrt_fusion
  (11 shorter events, 0.1 us)
Async XLA Ops:
  7.2 50.9 %copy-start.1 = (s32[64]{0:T(128)S(1)}, s32[64]{0:T(128)}, u32[]{:S(2)}) copy-start(s32[64]{0:T(128)} %param.7) | copy-start | bytes 772
  7.2 51.1 %copy-start = (s32[1,64,12]{1,0,2:T(1,128)S(1)}, s32[1,64,12]{1,0,2:T(1,128)}, u32[]{:S(2)}) copy-start(s32[1,64,12]{1,0,2:T(1,128)} %param.6) | copy-start | bytes 9220
  7.2 50.8 %all-gather.6.cloned.1.call-start = ((), (), s32[]{:S(2)}) async-start(), calls=%async_computation.2 | async-start | bytes 2621440 | tf_op jit(solution)/shard_map/all_gather | solution.py:32
  9.3 128.5 %all-gather.4.cloned.1.call-start = ((), (), s32[]{:S(2)}) async-start(), calls=%async_computation.1 | async-start | bytes 9175040 | tf_op jit(solution)/shard_map/all_gather | solution.py:34
  13.2 213.8 %all-gather.8.cloned.1.call-start = ((), (), s32[]{:S(2)}) async-start(), calls=%async_computation.3 | async-start | bytes 10485760 | tf_op jit(solution)/shard_map/all_gather | solution.py:35
  58.0 235.6 %reduce-scatter.2.cloned.1.call-start = ((), (), s32[]{:S(2)}) async-start(), calls=%async_computation.4 | async-start | bytes 28311552 | tf_op jit(solution)/shard_map/reduce_scatter | solution.py:49
Sparse Core Ops, SparseCore 0:
  9.6 48.3 all-gather.5
  60.4 77.4 all-gather.3
  139.7 87.3 all-gather.7
  267.0 26.5 reduce-scatter.1
where the time goes:
time: 307 us; the launch traced here: 305 us
  waiting for transfers between devices  161 us (52%)
  local copies, waits for them, and re-layouts  101 us (33%)
  matrix products  23.4 us (8%)
  between operations  13.9 us (5%)
  other arithmetic  6.12 us (2%)
    all_gather x1, waiting for transfers between devices, on_device(): hidden_piece = lax.all_gather(hidden, 'blk', axis=0, tiled=True)  78.1 us
    gather x2, local copies, waits for them, and re-layouts, on_device(): jnp.take(hidden_blocks, block_rows, axis=1)  67.6 us
    all_gather x1, waiting for transfers between devices, on_device(): grad_full = lax.all_gather(out_grad, 'team', axis=1, tiled=True)  44.7 us
    reduce_scatter x1, waiting for transfers between devices, on_device(): lax.psum_scatter(partial_value, 'dp', scatter_dimension=0, tiled=True)  26.7 us
    dot_general x1, matrix products, on_device(): jnp.einsum('ncki,ncj->ckij', picked_hidden, picked_grad, preferred_elemen...  23.4 us
    reshape x1, local copies, waits for them, and re-layouts, on_device(): grad_piece.reshape(count_rows, column_blocks, BS)  11.9 us
    all_gather x1, waiting for transfers between devices, on_device(): grad_piece = lax.all_gather(grad_full, 'blk', axis=0, tiled=True)  11.2 us
    reshape x1, local copies, waits for them, and re-layouts, on_device(): hidden_blocks = hidden_piece.reshape(count_rows, -1, BS)  10.4 us
  transfers between devices with their start and end apart: 4, of which 4 were waited for; matrix products, arithmetic and copies ran while one was open for 27% of the time, Pallas kernels for 0%

commit v1 on v0

--- a/solution.py
+++ b/solution.py
@@ -31,8 +31,11 @@
     block_rows = jnp.take(act_rows[0], owned_mine, axis=0).reshape(-1)
     grad_full = lax.all_gather(out_grad, "team", axis=1, tiled=True)
     grad_mask = alive_mine.astype(jnp.bfloat16)[None, :, None]
-    hidden_piece = lax.all_gather(hidden, "blk", axis=0, tiled=True)
-    grad_piece = lax.all_gather(grad_full, "blk", axis=0, tiled=True)
+    hidden_piece, grad_piece = jnp.split(
+        lax.all_gather(jnp.concatenate([hidden, grad_full], axis=1), "blk", tiled=True, axis=0),
+        [hidden.shape[1]],
+        axis=1,
+    )
     count_rows = grad_piece.shape[0]
     picked_grad = (
         jnp.take(grad_piece.reshape(count_rows, column_blocks, BS), owned_mine, axis=1) * grad_mask

time: 307 us -> 387 us (1.26)
  waiting for transfers between devices: 161 us -> 218 us
  local copies, waits for them, and re-layouts: 101 us -> 114 us
  other arithmetic: 6.12 us -> 15.4 us
    all_gather x2 -> x1, waiting for transfers between devices: 89.4 us -> 146 us  [on_device(): lax.all_gather(jnp.concatenate([hidden, grad_full], axis=1), 'blk', tiled...]
    split x0 -> x2, local copies, waits for them, and re-layouts: none -> 13.9 us  [on_device(): jnp.split(lax.all_gather(jnp.concatenate([hidden, grad_full], axis=1), 'b...]
    concatenate x0 -> x1, other arithmetic: none -> 9.28 us  [on_device(): jnp.concatenate([hidden, grad_full], axis=1)]
  transfers between devices with their start and end apart: 4 -> 3, of which waited for: 4 -> 3; matrix products, arithmetic and copies ran while one was open for 27% -> 1% of each run, Pallas kernels for 0% -> 0%
where the time goes in v1:
time: 387 us; the launch traced here: 385 us
  waiting for transfers between devices  218 us (56%)
  local copies, waits for them, and re-layouts  114 us (29%)
  matrix products  23.4 us (6%)
  other arithmetic  15.4 us (4%)
  between operations  13.9 us (4%)
    all_gather x1, waiting for transfers between devices, on_device(): lax.all_gather(jnp.concatenate([hidden, grad_full], axis=1), 'blk', tiled...  146 us
    gather x2, local copies, waits for them, and re-layouts, on_device(): jnp.take(hidden_blocks, block_rows, axis=1)  67.1 us
    all_gather x1, waiting for transfers between devices, on_device(): grad_full = lax.all_gather(out_grad, 'team', axis=1, tiled=True)  45.9 us
    reduce_scatter x1, waiting for transfers between devices, on_device(): lax.psum_scatter(partial_value, 'dp', scatter_dimension=0, tiled=True)  26.7 us
    dot_general x1, matrix products, on_device(): jnp.einsum('ncki,ncj->ckij', picked_hidden, picked_grad, preferred_elemen...  23.4 us
    split x2, local copies, waits for them, and re-layouts, on_device(): jnp.split(lax.all_gather(jnp.concatenate([hidden, grad_full], axis=1), 'b...  13.9 us
    reshape x1, local copies, waits for them, and re-layouts, on_device(): grad_piece.reshape(count_rows, column_blocks, BS)  11.9 us
    reshape x1, local copies, waits for them, and re-layouts, on_device(): hidden_blocks = hidden_piece.reshape(count_rows, -1, BS)  10.4 us
  transfers between devices with their start and end apart: 3, of which 3 were waited for; matrix products, arithmetic and copies ran while one was open for 1% of the time, Pallas kernels for 0%

profile of v1, /device:TPU:0, one launch (start us, length us, event | category | flops | bytes accessed | tf_op | source)
XLA Modules:
  0.0 385.1 jit_solution(18199390634600203848)
XLA Ops:
  7.2 0.0 all-gather.3.cloned.1.call-start
  7.2 2.0 copy.17
  9.3 0.0 all-gather.3.cloned.1.call-update
  9.3 0.0 copy-start
  9.3 0.0 all-gather.5.cloned.1.call-start
  9.3 3.3 copy.18
  12.7 45.9 %all-gather.3.cloned.1.call-done = bf16[128,8192]{0,1:T(8,128)(2,1)} async-done(((bf16[128,2048]{0,1:T(8,128)(2,1)}), bf16[128,8192]{0,1:T(8,128)(2,1)}) %all-gather.3.cloned.1.call-update) | async-done | bytes 2097168 | tf_op jit(solution)/shard_map/all_gather | solution.py:32
  58.5 9.3 %pad_maximum_fusion = bf16[128,15360]{0,1:T(8,128)(2,1)} fusion(bf16[128,8192]{0,1:T(8,128)(2,1)} %all-gather.3.cloned.1.call-done, bf16[128,7168]{0,1:T(8,128)(2,1)S(1)} %copy.18), kind=kLoop, calls=%fused_computation.8 | loop fusion | flops 7864320 | bytes 7864320 | tf_op jit(solution)/shard_map/concatenate | solution.py:35
  67.8 0.0 all-gather.5.cloned.1.call-update
  67.8 0.2 reduce-scatter.2.cloned.1.call-start
  68.1 0.1 copy.16
  68.2 0.1 fusion.11
  68.2 0.1 reduce_window_sum.11
  68.3 0.2 select_reduce_fusion
  68.6 0.1 fusion.10
  68.7 0.6 gather_fusion
  69.3 0.1 compare_and_fusion
  69.4 0.1 select_n.73
  69.5 0.2 and_reduce_fusion
  69.7 145.5 %all-gather.5.cloned.1.call-done = bf16[512,15360]{0,1:T(8,128)(2,1)} async-done(((bf16[128,15360]{0,1:T(8,128)(2,1)}), bf16[512,15360]{0,1:T(8,128)(2,1)}) %all-gather.5.cloned.1.call-update) | async-done | bytes 15728656 | tf_op jit(solution)/shard_map/all_gather | solution.py:35
  215.2 7.3 %split.9 = bf16[512,8192]{0,1:T(8,128)(2,1)} slice(bf16[512,15360]{0,1:T(8,128)(2,1)} %all-gather.5.cloned.1.call-done), slice={[0:512], [7168:15360]} | slice | bytes 16777216 | tf_op jit(solution)/shard_map/split | solution.py:34
  222.5 11.9 %copy.21 = bf16[512,64,128]{2,0,1:T(8,128)(2,1)} copy(bf16[512,64,128]{0,2,1:T(8,128)(2,1)} %bitcast.25) | data formatting | bytes 16777216 | tf_op jit(solution)/shard_map/reshape | solution.py:41
  234.5 4.5 %gather_fusion.2 = bf16[24,512,128]{2,1,0:T(8,128)(2,1)S(1)} fusion(bf16[512,64,128]{2,0,1:T(8,128)(2,1)} %copy.21, s32[1024]{0:T(1024)S(1)} %pad_clamp_fusion.1), kind=kCustom, calls=%fused_computation.2 | custom fusion | bytes 6291552 | tf_op jit(solution)/shard_map/jit(_take)/gather | solution.py:41
  239.0 6.6 %split.8 = bf16[512,7168]{0,1:T(8,128)(2,1)} slice(bf16[512,15360]{0,1:T(8,128)(2,1)} %all-gather.5.cloned.1.call-done), slice={[0:512], [0:7168]} | slice | bytes 14680064 | tf_op jit(solution)/shard_map/split | solution.py:34
  245.6 10.4 %copy.19 = bf16[512,56,128]{2,0,1:T(8,128)(2,1)} copy(bf16[512,56,128]{0,2,1:T(8,128)(2,1)} %bitcast.26) | data formatting | bytes 14680064 | tf_op jit(solution)/shard_map/reshape | solution.py:44
  256.0 18.4 %gather_fusion.1 = bf16[288,512,128]{2,1,0:T(8,128)(2,1)} fusion(bf16[512,56,128]{2,0,1:T(8,128)(2,1)} %copy.19, s32[1024]{0:T(1024)S(1)} %pad_clamp_fusion), kind=kCustom, calls=%fused_computation.1 | custom fusion | bytes 75498624 | tf_op jit(solution)/shard_map/jit(_take)/gather | solution.py:45
  274.4 48.7 %copy.20 = bf16[512,24,12,128]{0,3,2,1:T(8,128)(2,1)} copy(bf16[512,24,12,128]{3,0,2,1:T(8,128)(2,1)} %bitcast.24) | data formatting | bytes 75497472 | tf_op jit(solution)/shard_map/jit(_take)/gather | solution.py:45
  323.1 23.4 %fusion = f32[24,12,128,128]{3,2,1,0:T(8,128)} fusion(bf16[512,24,12,128]{0,3,2,1:T(8,128)(2,1)} %copy.20, pred[24,12]{1,0:T(8,128)(4,1)S(1)} %get-tuple-element.2, bf16[24,512,128]{2,1,0:T(8,128)(2,1)S(1)} %gather_fusion.2, pred[24]{0:T(512)(128)(4,1)S(1)} %compare_and_fusion.1, bf16[24]{0:T(256)(128)(2,1)S(1)} %fusion.13), kind=kOutput, calls=%fused_computation.3 | convolution fusion | flops 4853858304 | bytes 59769192 | tf_op jit(solution)/shard_map/ncki,ncj->ckij/dot_general | solution.py:48
  346.5 0.0 reduce-scatter.2.cloned.1.call-update
  346.5 26.7 %reduce-scatter.2.cloned.1.call-done = f32[144,128,128]{2,1,0:T(8,128)} async-done(((f32[288,128,128]{2,1,0:T(8,128)}), f32[144,128,128]{2,1,0:T(8,128)}) %reduce-scatter.2.cloned.1.call-update) | async-done | bytes 9437200 | tf_op jit(solution)/shard_map/reduce_scatter | solution.py:52
  373.3 4.7 %multiply_reduce_fusion = f32[144]{0:T(256)S(1)} fusion(f32[144,128,128]{2,1,0:T(8,128)} %reduce-scatter.2.cloned.1.call-done), kind=kLoop, calls=%fused_computation.7 | loop fusion | flops 4718448 | bytes 9437760 | tf_op jit(solution)/shard_map/reduce_sum | solution.py:53
  378.0 0.6 add_sqrt_fusion
  (11 shorter events, 0.1 us)
Async XLA Ops:
  7.2 51.4 %all-gather.3.cloned.1.call-start = ((), (), s32[]{:S(2)}) async-start(), calls=%async_computation.1 | async-start | bytes 2621440 | tf_op jit(solution)/shard_map/all_gather | solution.py:32
  9.3 58.8 %copy-start = (s32[1,64,12]{1,0,2:T(1,128)S(1)}, s32[1,64,12]{1,0,2:T(1,128)}, u32[]{:S(2)}) copy-start(s32[1,64,12]{1,0,2:T(1,128)} %param.6) | copy-start | bytes 9220
  9.3 58.9 %copy-start.1 = (s32[64]{0:T(128)S(1)}, s32[64]{0:T(128)}, u32[]{:S(2)}) copy-start(s32[64]{0:T(128)} %param.7) | copy-start | bytes 772
  9.3 205.9 %all-gather.5.cloned.1.call-start = ((), (), s32[]{:S(2)}) async-start(), calls=%async_computation.2 | async-start | bytes 19660800 | tf_op jit(solution)/shard_map/all_gather | solution.py:35
  67.8 305.4 %reduce-scatter.2.cloned.1.call-start = ((), (), s32[]{:S(2)}) async-start(), calls=%async_computation.3 | async-start | bytes 28311552 | tf_op jit(solution)/shard_map/reduce_scatter | solution.py:52
Sparse Core Ops, SparseCore 0:
  10.1 48.3 all-gather.2
  68.0 147.2 all-gather.4
  346.6 26.5 reduce-scatter.1
